TPU v7x, 128 devices: a whole 4x4x4 slice. The times are simulated.
128 devices in a mesh: lat: 16 (over x, y), var: 8 (over z, core).
Axes of the slice: x: 4, y: 4, z: 4, core: 2. Of those that a mesh axis runs over, the one named last changes fastest.
Arguments:
- patches: bfloat16 [96, 192, 1024], P('lat', 'var'), may hold values from -6 to 6
- norm_gain: float32 [1024], replicated, may hold values from 0.25 to 1.75
- input_proj: bfloat16 [1024, 3072], replicated, may hold values from -7 to 7
- output_proj: bfloat16 [1024, 1024], replicated, may hold values from -0.1875 to 0.1875
- level_scale: float32 [40, 1024], P('var'), may hold values from 0.1 to 1.9
- level_shift: float32 [40, 1024], P('var'), may hold values from -3 to 3
- head_weight: bfloat16 [40, 1024, 320], P('var', 'lat'), may hold values from -0.1875 to 0.1875
- targets: bfloat16 [40, 96, 192, 320], P('var', 'lat'), may hold values from -6 to 6
- level_counts: int32 [4], replicated, may hold values from 13 to 37
- tile_dataset: int32 [16, 8], P('lat'), may hold values from 0 to 3
- slot_level: int32 [40], P('var'), may hold values from 0 to 39, as said below
Outputs:
- latent: bfloat16 [96, 192, 1024], P('lat', 'var')
- grad_latent: bfloat16 [96, 192, 1024], P('lat', 'var')
- grad_head: float32 [40, 1024, 320], P('var', 'lat')
Inputs may be any that keep to these rules, and one draw needn't show every extreme that they name: `slot_level`: for each j, slots j * 5 to (j + 1) * 5 - 1 hold the levels j * 5 to (j + 1) * 5 - 1 in some order.
All inputs are finite; a program needn't handle non-finite values.
Results may differ from a plain program's by a relative error of at most 0.012.
Values may be sent and summed in bfloat16 or wider, within the bound.
A program may use at most 128 MiB of HBM per device.

v0:
```python
import math
import jax
import jax.numpy as jnp
from jax import lax
from jax.sharding import PartitionSpec as P

HEADS = 16
WH = 6
WW = 12
EPS = 1e-05


def padded(array, sides, width, wrap):
    for axis, dim in sides:
        size, length = (lax.axis_size(axis), array.shape[dim])
        up = [(i, (i + 1) % size) for i in range(size if wrap else size - 1)]
        down = [(j, i) for i, j in up]
        last = lax.slice_in_dim(array, length - width, length, axis=dim)
        initial = lax.slice_in_dim(array, 0, width, axis=dim)
        before = lax.ppermute(last, axis, up)
        after = lax.ppermute(initial, axis, down)
        array = jnp.concatenate([before, array, after], axis=dim)
    return array


def layer_norm(values, gain):
    wide = values.astype(jnp.float32)
    average = jnp.mean(wide, axis=-1, keepdims=True)
    centred = wide - average
    variance = jnp.mean(centred * centred, axis=-1, keepdims=True)
    return (centred * lax.rsqrt(variance + EPS) * gain).astype(jnp.bfloat16)


def window_attention(query_ext, keyval, row_valid, heads):
    ext_rows, ext_cols, width = query_ext.shape
    head_size = width // heads
    win_rows = ext_rows // WH
    win_cols = ext_cols // WW

    def split(values, parts):
        shaped = values.reshape(win_rows, WH, win_cols, WW, parts, heads, head_size)
        return shaped.transpose(0, 2, 1, 3, 4, 5, 6).reshape(
            win_rows * win_cols, WH * WW, parts, heads, head_size
        )

    query_win = split(query_ext, 1)[:, :, 0]
    pairs = split(keyval, 2)
    key_win = pairs[:, :, 0]
    value_win = pairs[:, :, 1]
    key_mask = jnp.broadcast_to(
        row_valid.reshape(win_rows, 1, WH, 1), (win_rows, win_cols, WH, WW)
    ).reshape(win_rows * win_cols, WH * WW)
    scores = jnp.einsum(
        "wqhd,wkhd->whqk", query_win, key_win, preferred_element_type=jnp.float32
    ) / math.sqrt(head_size)
    scores = jnp.where(key_mask[:, None, None, :], scores, -jnp.inf)
    peak = jnp.max(scores, axis=-1, keepdims=True)
    weights = jnp.exp(scores - peak)
    probs = (weights / jnp.sum(weights, axis=-1, keepdims=True)).astype(jnp.bfloat16)
    mixed = jnp.einsum("whqk,wkhd->wqhd", probs, value_win, preferred_element_type=jnp.float32)
    return (
        mixed.reshape(win_rows, win_cols, WH, WW, width)
        .transpose(0, 2, 1, 3, 4)
        .reshape(ext_rows, ext_cols, width)
    )


def slot_terms(piece, target_rows, live_cols, level_scale, level_shift, heads_full):
    piece_wide = piece.astype(jnp.float32)
    rows = (
        piece_wide[None] * level_scale[:, None, None, :] + level_shift[:, None, None, :]
    ).astype(jnp.bfloat16)
    predicted = jnp.einsum("krnd,kdo->krno", rows, heads_full, preferred_element_type=jnp.float32)
    errors = ((predicted - target_rows.astype(jnp.float32)) * live_cols[:, None, :, None]).astype(
        jnp.bfloat16
    )
    back_grad = jnp.einsum("krno,kdo->krnd", errors, heads_full, preferred_element_type=jnp.float32)
    piece_grad = jnp.sum(back_grad * level_scale[:, None, None, :], axis=0)
    head_add = jnp.einsum("krnd,krno->dko", rows, errors, preferred_element_type=jnp.float32)
    return (piece_grad, head_add)


def local(
    patches,
    norm_gain,
    input_proj,
    output_proj,
    level_scale,
    level_shift,
    head_weight,
    targets,
    level_counts,
    tile_dataset,
    slot_level,
):
    band_rows, band_cols, width = patches.shape
    half_rows = WH // 2
    half_cols = WW // 2
    lat_count = lax.axis_size("lat")
    var_count = lax.axis_size("var")
    lat_place = lax.axis_index("lat")
    ext_rows = band_rows + WH
    ext_cols = band_cols + WW
    extended = padded(patches, (("lat", 0),), half_rows, False)
    extended = padded(extended, (("var", 1),), half_cols, True)
    normed_ext = layer_norm(extended, norm_gain)
    keyval = jnp.dot(
        normed_ext.reshape(-1, width), input_proj[:, width:], preferred_element_type=jnp.float32
    )
    keyval = keyval.astype(jnp.bfloat16).reshape(ext_rows, ext_cols, 2 * width)
    normed = normed_ext[half_rows : half_rows + band_rows, half_cols : half_cols + band_cols]
    queries = jnp.dot(
        normed.reshape(-1, width), input_proj[:, :width], preferred_element_type=jnp.float32
    )
    queries = queries.astype(jnp.bfloat16).reshape(band_rows, band_cols, width)
    query_ext = jnp.pad(queries, ((half_rows, WH - half_rows), (half_cols, WW - half_cols), (0, 0)))
    global_row = lat_place * band_rows - half_rows + jnp.arange(ext_rows, dtype=jnp.int32)
    row_valid = (global_row >= 0) & (global_row < lat_count * band_rows)
    mixed = window_attention(query_ext, keyval, row_valid, HEADS)
    attn = mixed[half_rows : half_rows + band_rows, half_cols : half_cols + band_cols].astype(
        jnp.bfloat16
    )
    update = jnp.dot(
        attn.reshape(-1, width), output_proj, preferred_element_type=jnp.float32
    ).reshape(band_rows, band_cols, width)
    latent = (patches.astype(jnp.float32) + update).astype(jnp.bfloat16)
    dataset_row = tile_dataset[0]
    dataset_ids = jnp.arange(level_counts.shape[0], dtype=jnp.int32)
    tile_levels = jnp.sum(
        jnp.where(dataset_row[:, None] == dataset_ids[None, :], level_counts[None, :], 0), axis=1
    )
    live_tiles = (slot_level[None, :] < tile_levels[:, None]).astype(jnp.float32)
    heads_full = lax.all_gather(head_weight, "lat", axis=1, tiled=True)
    tile_ids = jnp.arange(var_count, dtype=jnp.int32)
    piece = lax.all_gather(latent, "var", axis=1, tiled=True)
    piece_cols = piece.shape[1]
    column_tile = jnp.arange(piece_cols, dtype=jnp.int32) // band_cols
    onehot = (column_tile[:, None] == tile_ids[None, :]).astype(jnp.float32)
    column_live = jnp.dot(onehot, live_tiles)
    piece_grad, head_add = slot_terms(
        piece, targets, column_live.T, level_scale, level_shift, heads_full
    )
    latent_terms = piece_grad
    latent_terms, head_terms = (latent_terms, head_add)
    grad_latent = lax.psum_scatter(
        latent_terms.astype(jnp.bfloat16), "var", scatter_dimension=1, tiled=True
    )
    head_terms = head_terms * (1.0 / math.sqrt(lat_count * band_rows * var_count * band_cols))
    share_rows = width // lat_count
    summed = lax.psum(head_terms.astype(jnp.bfloat16), "lat").astype(jnp.float32)
    mine = lax.dynamic_slice_in_dim(summed, lat_place * share_rows, share_rows, 0)
    grad_head = jnp.transpose(mine, (1, 0, 2))
    return (latent, grad_latent, grad_head)


def solution(mesh):
    in_specs = (
        P("lat", "var", None),
        P(),
        P(),
        P(),
        P("var", None),
        P("var", None),
        P("var", "lat", None),
        P("var", "lat", None, None),
        P(),
        P("lat", None),
        P("var"),
    )
    out_specs = (P("lat", "var", None), P("lat", "var", None), P("var", "lat", None))
    return jax.shard_map(local, mesh=mesh, in_specs=in_specs, out_specs=out_specs, check_vma=False)
```

profile of v0, /device:TPU:0, one launch (start us, length us, event | category | flops | bytes accessed | tf_op | source)
XLA Modules:
  0.0 327.8 jit_solution(17000856274102400193)
XLA Ops:
  7.2 0.0 copy-start
  7.2 0.0 all-gather.3.cloned.1.call-start
  7.2 1.1 fusion.61
  8.4 3.6 %collective-permute-start = (bf16[3,24,1024]{2,1,0:T(8,128)(2,1)S(1)}, bf16[3,24,1024]{2,1,0:T(8,128)(2,1)S(1)}, u32[]{:S(2)}, u32[]{:S(2)}) collective-permute-start(bf16[3,24,1024]{2,1,0:T(8,128)(2,1)S(1)} %get-tuple-element.25), channel_id=1, source_target_pairs={{0,8},{8,16},{16,24},{24,32},{32,40},{40,48},{48,56},{56,64},{64,7... | collective-permute-start | bytes 442376 | tf_op jit(solution)/shard_map/ppermute | solution.py:20
  12.0 1.3 collective-permute-start.1
  13.3 1.8 collective-permute-done
  15.0 1.0 constant_dynamic-update-slice_fusion.1
  16.0 3.1 collective-permute-done.1
  19.2 0.1 fusion.60
  19.2 0.0 collective-permute-start.2
  19.3 2.9 collective-permute-start.3
  22.2 0.1 broadcast_in_dim.28
  22.3 0.1 broadcast_in_dim.29
  22.4 3.2 collective-permute-done.2
  25.6 0.4 fusion.58
  26.0 0.1 div.33
  26.1 1.9 multiply_reduce_fusion.1
  28.0 0.1 rsqrt.13
  28.0 0.1 slice.45
  28.1 1.6 maximum_convert_fusion
  29.8 2.6 reshape.102
  32.4 1.3 fusion.50
  33.7 2.1 fusion.40
  35.8 0.2 pad.4
  35.9 2.1 reshape.99
  38.0 3.2 copy.47
  41.2 5.5 %fusion.15 = bf16[432,2048]{1,0:T(8,128)(2,1)} fusion(bf16[1024,3072]{1,0:T(8,128)(2,1)} %param.13, f32[432,1024]{1,0:T(8,128)S(1)} %copy-done.3, f32[1024]{0:T(1024)S(1)} %copy-done.5, f32[432]{0:T(512)S(1)} %rsqrt.13, f32[432]{0:T(512)S(1)} %div.33), kind=kOutput, calls=%fused_computation.22 | convolution fusion | flops 1814593536 | bytes 7740800 | tf_op jit(solution)/shard_map/dot_general | solution.py:107
  46.8 6.4 %reshape_reshape.3 = bf16[2,6,3,12,2,16,64]{6,5,4,3,2,1,0:T(8,128)(2,1)} reshape(bf16[432,2048]{1,0:T(8,128)(2,1)} %fusion.15) | data formatting | bytes 3538944 | tf_op jit(solution)/shard_map/reshape;reshape | solution.py:41
  53.1 2.6 copy.45
  55.8 2.7 fusion.59
  58.4 4.0 %copy.59 = bf16[6,72,1,16,64]{1,4,3,0,2:T(8,128)(2,1)} copy(bf16[6,72,1,16,64]{4,3,2,1,0:T(8,128)(2,1)} %get-tuple-element.18) | data formatting | bytes 1769472
  62.5 4.0 %copy.60 = bf16[6,72,1,16,64]{1,4,3,0,2:T(8,128)(2,1)} copy(bf16[6,72,1,16,64]{4,3,2,1,0:T(8,128)(2,1)} %get-tuple-element.19) | data formatting | bytes 1769472
  66.5 3.1 fusion.25
  69.6 1.8 fusion.62
  71.4 1.9 fusion.34
  73.3 4.0 %copy.51 = bf16[6,72,16,64]{3,2,1,0:T(8,128)(2,1)} copy(bf16[6,72,16,64]{1,3,2,0:T(8,128)(2,1)} %fusion.34) | data formatting | bytes 1769472 | tf_op jit(solution)/shard_map/whqk,wkhd->wqhd/transpose | solution.py:60
  77.3 3.9 %reshape.100 = bf16[2,3,6,12,1024]{4,3,2,1,0:T(8,128)(2,1)} reshape(bf16[6,72,16,64]{3,2,1,0:T(8,128)(2,1)} %copy.51) | data formatting | bytes 1769472 | tf_op jit(solution)/shard_map/reshape | solution.py:62
  81.2 1.4 copy.52
  82.6 0.0 copy-start.9
  82.6 1.0 reshape.101
  83.7 2.3 fusion.43
  86.0 0.0 all-gather.3.cloned.1.call-update
  86.0 0.0 all-gather.5.cloned.1.call-start
  86.0 0.7 all-gather.5.cloned.1.call-update
  86.7 0.0 all-reduce.3.cloned.1.call-start
  86.8 0.1 select_reduce_fusion
  86.9 0.2 fusion.52
  87.1 28.4 %all-gather.3.cloned.1.call-done = bf16[6,192,1024]{2,1,0:T(8,128)(2,1)} async-done(((bf16[6,24,1024]{2,1,0:T(8,128)(2,1)}), bf16[6,192,1024]{2,1,0:T(8,128)(2,1)}) %all-gather.3.cloned.1.call-update) | async-done | bytes 2359312 | tf_op jit(solution)/shard_map/all_gather | solution.py:135
  115.6 4.4 %convert_element_type.69 = f32[6,192,1024]{2,1,0:T(8,128)} convert(bf16[6,192,1024]{2,1,0:T(8,128)(2,1)} %all-gather.3.cloned.1.call-done) | non-fusion elementwise | flops 1179648 | bytes 7077888 | tf_op jit(solution)/shard_map/convert_element_type | solution.py:69
  119.9 48.6 %all-gather.5.cloned.1.call-done = bf16[5,1024,320]{2,1,0:T(8,128)(2,1)} async-done(((bf16[5,64,320]{2,1,0:T(8,128)(2,1)}), bf16[5,1024,320]{2,1,0:T(8,128)(2,1)}) %all-gather.5.cloned.1.call-update) | async-done | bytes 3276816 | tf_op jit(solution)/shard_map/all_gather | solution.py:133
  168.5 10.1 %multiply_convert_fusion = bf16[5,6,192,320]{3,2,1,0:T(8,128)(2,1)S(1)} fusion(bf16[5,6,192,320]{3,2,1,0:T(8,128)(2,1)} %param.18, f32[5,192]{1,0:T(8,128)S(1)} %fusion.52, bf16[5,1024,320]{2,1,0:T(8,128)(2,1)} %all-gather.5.cloned.1.call-done, f32[5,1024]{1,0:T(8,128)S(1)} %copy-done.6, f32[5,1024]{1,0:T(8,128)S(1)} %copy-done.7, ...), kind=kOutput, calls=%fused_computation.11 | convolution fusion | flops 3799941120 | bytes 15412992 | tf_op jit(solution)/shard_map/krnd,kdo->krno/dot_general | solution.py:73
  178.6 2.1 copy-done.11
  180.8 6.6 %fusion.14 = bf16[1024,5,320]{0,2,1:T(8,128)(2,1)} fusion(bf16[5,6,192,320]{3,2,1,0:T(8,128)(2,1)S(1)} %multiply_convert_fusion, f32[5,1024]{1,0:T(8,128)S(1)} %copy-done.6, f32[5,1024]{1,0:T(8,128)S(1)} %copy-done.7, f32[6,192,1024]{2,1,0:T(8,128)S(1)} %copy-done.2), kind=kOutput, calls=%fused_computation.21 | convolution fusion | flops 3795845120 | bytes 11722752 | tf_op jit(solution)/shard_map/krnd,krno->dko/dot_general | solution.py:79
  187.4 0.0 all-reduce.3.cloned.1.call-update
  187.4 0.0 reduce-scatter.4.cloned.1.call-start
  187.5 9.9 %multiply_reduce_fusion = bf16[6,192,1024]{2,1,0:T(8,128)(2,1)S(1)} fusion(f32[5,1024]{1,0:T(8,128)S(1)} %copy-done.7, bf16[5,6,192,320]{3,2,1,0:T(8,128)(2,1)} %copy-done.11, bf16[5,1024,320]{2,1,0:T(8,128)(2,1)} %all-gather.5.cloned.1.call-done), kind=kOutput, calls=%fused_computation.1 | convolution fusion | flops 3785490432 | bytes 9342976 | tf_op jit(solution)/shard_map/krno,kdo->krnd/dot_general | solution.py:77
  197.4 1.7 copy.61
  199.0 0.0 reduce-scatter.4.cloned.1.call-update
  199.1 84.3 %all-reduce.3.cloned.1.call-done = bf16[1024,5,320]{0,2,1:T(8,128)(2,1)} async-done(((bf16[1024,5,320]{0,2,1:T(8,128)(2,1)}), bf16[1024,5,320]{0,2,1:T(8,128)(2,1)}) %all-reduce.3.cloned.1.call-update) | async-done | bytes 3276816 | tf_op jit(solution)/shard_map/psum | solution.py:150
  283.3 1.2 convert_bitcast_fusion
  284.5 1.1 copy.53
  285.6 33.4 %reduce-scatter.4.cloned.1.call-done = bf16[24,6144]{1,0:T(8,128)(2,1)} async-done(((bf16[192,6144]{1,0:T(8,128)(2,1)}), bf16[24,6144]{1,0:T(8,128)(2,1)}) %reduce-scatter.4.cloned.1.call-update) | async-done | bytes 294928
  319.1 1.3 reshape.107
  320.4 0.9 copy.58
  (28 shorter events, 0.1 us)
Async XLA Ops:
  7.2 76.5 %copy-start = (bf16[1024,1024]{1,0:T(8,128)(2,1)S(1)}, bf16[1024,1024]{1,0:T(8,128)(2,1)}, u32[]{:S(2)}) copy-start(bf16[1024,1024]{1,0:T(8,128)(2,1)} %param.14) | copy-start | bytes 6291460
  7.2 108.4 %all-gather.3.cloned.1.call-start = ((), (), s32[]{:S(2)}) async-start(), calls=%async_computation.1 | async-start | bytes 2654208 | tf_op jit(solution)/shard_map/all_gather | solution.py:135
  8.4 6.7 %collective-permute-start = (bf16[3,24,1024]{2,1,0:T(8,128)(2,1)S(1)}, bf16[3,24,1024]{2,1,0:T(8,128)(2,1)S(1)}, u32[]{:S(2)}, u32[]{:S(2)}) collective-permute-start(bf16[3,24,1024]{2,1,0:T(8,128)(2,1)S(1)} %get-tuple-element.25), channel_id=1, source_target_pairs={{0,8},{8,16},{16,24},{24,32},{32,40},{40,48},{48,56},{56,64},{64,7... | collective-permute-start | bytes 442376 | tf_op jit(solution)/shard_map/ppermute | solution.py:20
  12.0 7.2 %collective-permute-start.1 = (bf16[3,24,1024]{2,1,0:T(8,128)(2,1)S(1)}, bf16[3,24,1024]{2,1,0:T(8,128)(2,1)S(1)}, u32[]{:S(2)}, u32[]{:S(2)}) collective-permute-start(bf16[3,24,1024]{2,1,0:T(8,128)(2,1)S(1)} %get-tuple-element.24), channel_id=1, source_target_pairs={{8,0},{16,8},{24,16},{32,24},{40,32},{48,40},{56,48},{64,56},{72,6... | collective-permute-start | bytes 442376 | tf_op jit(solution)/shard_map/ppermute | solution.py:21
  19.2 6.3 %collective-permute-start.2 = (bf16[12,6,1024]{2,1,0:T(8,128)(2,1)S(1)}, bf16[12,6,1024]{2,1,0:T(8,128)(2,1)S(1)}, u32[]{:S(2)}, u32[]{:S(2)}) collective-permute-start(bf16[12,6,1024]{2,1,0:T(8,128)(2,1)S(1)} %get-tuple-element.22), channel_id=1, source_target_pairs={{0,1},{1,2},{2,3},{3,4},{4,5},{5,6},{6,7},{7,0},{8,9},{9,10},{10,1... | collective-permute-start | bytes 442376 | tf_op jit(solution)/shard_map/ppermute | solution.py:20
  19.3 6.3 %collective-permute-start.3 = (bf16[12,6,1024]{2,1,0:T(8,128)(2,1)S(1)}, bf16[12,6,1024]{2,1,0:T(8,128)(2,1)S(1)}, u32[]{:S(2)}, u32[]{:S(2)}) collective-permute-start(bf16[12,6,1024]{2,1,0:T(8,128)(2,1)S(1)} %get-tuple-element.23), channel_id=1, source_target_pairs={{1,0},{2,1},{3,2},{4,3},{5,4},{6,5},{7,6},{0,7},{9,8},{10,9},{11,1... | collective-permute-start | bytes 442376 | tf_op jit(solution)/shard_map/ppermute | solution.py:21
  27.9 4.4 %copy-start.5 = (f32[1024]{0:T(1024)S(1)}, f32[1024]{0:T(1024)}, u32[]{:S(2)}) copy-start(f32[1024]{0:T(1024)} %param.12) | copy-start | bytes 12292
  38.0 3.2 copy-start.3
  69.6 1.8 copy-start.4
  82.6 4.2 %copy-start.8 = (s32[4]{0:T(128)S(1)}, s32[4]{0:T(128)}, u32[]{:S(2)}) copy-start(s32[4]{0:T(128)} %param.19) | copy-start | bytes 52
  82.6 4.2 %copy-start.9 = (s32[1,8]{1,0:T(1,128)S(1)}, s32[1,8]{1,0:T(1,128)}, u32[]{:S(2)}) copy-start(s32[1,8]{1,0:T(1,128)} %param.20) | copy-start | bytes 100
  82.6 4.3 %copy-start.10 = (s32[5]{0:T(128)S(1)}, s32[5]{0:T(128)}, u32[]{:S(2)}) copy-start(s32[5]{0:T(128)} %param.21) | copy-start | bytes 64
  86.0 82.5 %all-gather.5.cloned.1.call-start = ((), (), s32[]{:S(2)}) async-start(), calls=%async_computation.2 | async-start | bytes 4177920 | tf_op jit(solution)/shard_map/all_gather | solution.py:133
  86.7 196.6 %all-reduce.3.cloned.1.call-start = ((), (), s32[]{:S(2)}) async-start(), calls=%async_computation.3 | async-start | bytes 6553600 | tf_op jit(solution)/shard_map/psum | solution.py:150
  87.1 81.4 %copy-start.6 = (f32[5,1024]{1,0:T(8,128)S(1)}, f32[5,1024]{1,0:T(8,128)}, u32[]{:S(2)}) copy-start(f32[5,1024]{1,0:T(8,128)} %param.16) | copy-start | bytes 61444
  87.1 81.4 %copy-start.7 = (f32[5,1024]{1,0:T(8,128)S(1)}, f32[5,1024]{1,0:T(8,128)}, u32[]{:S(2)}) copy-start(f32[5,1024]{1,0:T(8,128)} %param.15) | copy-start | bytes 61444
  168.5 12.3 %copy-start.2 = (f32[6,192,1024]{2,1,0:T(8,128)S(1)}, f32[6,192,1024]{2,1,0:T(8,128)}, u32[]{:S(2)}) copy-start(f32[6,192,1024]{2,1,0:T(8,128)} %convert_element_type.69) | copy-start | bytes 14155780
  178.6 2.2 copy-start.11
  187.4 131.6 %reduce-scatter.4.cloned.1.call-start = ((), (), s32[]{:S(2)}) async-start(), calls=%async_computation.4 | async-start | bytes 2654208
  197.4 123.9 %copy-start.1 = (bf16[1024,1024]{1,0:T(8,128)(2,1)S(1)}, bf16[1024,1024]{1,0:T(8,128)(2,1)}, u32[]{:S(2)}) copy-start(bf16[1024,1024]{1,0:T(8,128)(2,1)} %param.14) | copy-start | bytes 6291460
Sparse Core Ops, SparseCore 0:
  86.1 29.4 all-gather.2
  117.7 50.7 all-gather.4
  187.6 95.7 all-reduce.2
  285.8 33.2 reduce-scatter.3
where the time goes:
time: 329 us; the launch traced here: 328 us
  waiting for transfers between devices  204 us (62%)
  local copies, waits for them, and re-layouts  48 us (15%)
  matrix products  41.6 us (13%)
  between operations  14 us (4%)
  other arithmetic  12.7 us (4%)
  starting transfers between devices  7.98 us (2%)
    psum x1, waiting for transfers between devices, local(): lax.psum(head_terms.astype(jnp.bfloat16), 'lat').astype(jnp.float32)  84.3 us
    all_gather x1, waiting for transfers between devices, local(): heads_full = lax.all_gather(head_weight, 'lat', axis=1, tiled=True)  48.6 us
    unnamed x5, waiting for transfers between devices  34.2 us
    all_gather x1, waiting for transfers between devices, local(): piece = lax.all_gather(latent, 'var', axis=1, tiled=True)  28.4 us
    unnamed x32, local copies, waits for them, and re-layouts  16.3 us
    dot_general x1, matrix products, slot_terms(): jnp.einsum('krnd,kdo->krno', rows, heads_full, preferred_element_type=jnp...  10.1 us
    dot_general x1, matrix products, slot_terms(): jnp.einsum('krno,kdo->krnd', errors, heads_full, preferred_element_type=j...  9.86 us
    another operation x2, local copies, waits for them, and re-layouts, split(): shaped = values.reshape(win_rows, WH, win_cols, WW, parts, heads, head_size)  8.98 us
  transfers between devices with their start and end apart: 8, of which 7 were waited for; matrix products, arithmetic and copies ran while one was open for 6% of the time, Pallas kernels for 0%

commit v1 on v0

--- a/solution.py
+++ b/solution.py
@@ -132,7 +132,24 @@
     live_tiles = (slot_level[None, :] < tile_levels[:, None]).astype(jnp.float32)
     heads_full = lax.all_gather(head_weight, "lat", axis=1, tiled=True)
     tile_ids = jnp.arange(var_count, dtype=jnp.int32)
-    piece = lax.all_gather(latent, "var", axis=1, tiled=True)
+    peers, index, rows_2 = (lax.axis_size("var"), lax.axis_index("var"), latent.shape[1])
+    ahead = [(i_2, (i_2 + 1) % peers) for i_2 in range(peers)]
+    backward = [(i_2, (i_2 - 1) % peers) for i_2 in range(peers)]
+    out = jnp.zeros((*latent.shape[:1], peers * rows_2, *latent.shape[1 + 1 :]), latent.dtype)
+    out = lax.dynamic_update_slice_in_dim(out, latent, index * rows_2, axis=1)
+    from_left = from_right = latent
+    half = peers // 2
+    for step in range(1, half + 1):
+        from_left = lax.ppermute(from_left, "var", ahead)
+        out = lax.dynamic_update_slice_in_dim(
+            out, from_left, (index - step) % peers * rows_2, axis=1
+        )
+        if step < peers - half:
+            from_right = lax.ppermute(from_right, "var", backward)
+            out = lax.dynamic_update_slice_in_dim(
+                out, from_right, (index + step) % peers * rows_2, axis=1
+            )
+    piece = out
     piece_cols = piece.shape[1]
     column_tile = jnp.arange(piece_cols, dtype=jnp.int32) // band_cols
     onehot = (column_tile[:, None] == tile_ids[None, :]).astype(jnp.float32)

time: 329 us -> 283 us (0.86)
  waiting for transfers between devices: 204 us -> 142 us
  starting transfers between devices: 7.98 us -> 16.9 us
  local copies, waits for them, and re-layouts: 48 us -> 55.1 us
    all_gather x1, waiting for transfers between devices: 48.6 us -> 0.01 us  [local(): heads_full = lax.all_gather(head_weight, 'lat', axis=1, tiled=True)]
    all_gather x1 -> x0, waiting for transfers between devices: 28.4 us -> none  [local(): piece = lax.all_gather(latent, 'var', axis=1, tiled=True)]
    ppermute x0 -> x7, waiting for transfers between devices: none -> 15.7 us  [the longest x4 15.7 us: local(): from_left = lax.ppermute(from_left, 'var', ahead)]
    ppermute x0 -> x7, starting transfers between devices: none -> 8.91 us  [the longest x3 8.16 us: local(): from_right = lax.ppermute(from_right, 'var', backward)]
    dynamic_update_slice x0 -> x7, local copies, waits for them, and re-layouts: none -> 5.22 us  [the longest x4 3 us: local(): lax.dynamic_update_slice_in_dim(out, from_left, (index - step) % peers *...]
    unnamed x5 -> x4, waiting for transfers between devices: 34.2 us -> 33.6 us
    unnamed x32 -> x36, local copies, waits for them, and re-layouts: 16.3 us -> 16.2 us
  transfers between devices with their start and end apart: 8 -> 14, of which waited for: 7 -> 9; matrix products, arithmetic and copies ran while one was open for 6% -> 31% of each run, Pallas kernels for 0% -> 0%
where the time goes in v1:
time: 283 us; the launch traced here: 282 us
  waiting for transfers between devices  142 us (50%)
  local copies, waits for them, and re-layouts  55.1 us (19%)
  matrix products  41.5 us (15%)
  starting transfers between devices  16.9 us (6%)
  between operations  14 us (5%)
  other arithmetic  12.6 us (4%)
    psum x1, waiting for transfers between devices, local(): lax.psum(head_terms.astype(jnp.bfloat16), 'lat').astype(jnp.float32)  84.8 us
    unnamed x4, waiting for transfers between devices  33.6 us
    unnamed x36, local copies, waits for them, and re-layouts  16.2 us
    ppermute x4, waiting for transfers between devices, local(): from_left = lax.ppermute(from_left, 'var', ahead)  15.7 us
    dot_general x1, matrix products, slot_terms(): jnp.einsum('krnd,kdo->krno', rows, heads_full, preferred_element_type=jnp...  9.92 us
    dot_general x1, matrix products, slot_terms(): jnp.einsum('krno,kdo->krnd', errors, heads_full, preferred_element_type=j...  9.86 us
    another operation x2, local copies, waits for them, and re-layouts, split(): shaped = values.reshape(win_rows, WH, win_cols, WW, parts, heads, head_size)  9.05 us
    ppermute x3, starting transfers between devices, local(): from_right = lax.ppermute(from_right, 'var', backward)  8.16 us
  transfers between devices with their start and end apart: 14, of which 9 were waited for; matrix products, arithmetic and copies ran while one was open for 31% of the time, Pallas kernels for 0%

profile of v1, /device:TPU:0, one launch (start us, length us, event | category | flops | bytes accessed | tf_op | source)
XLA Modules:
  0.0 282.3 jit_solution(10976318225025307687)
XLA Ops:
  7.2 1.1 fusion.61
  8.4 3.6 %collective-permute-start = (bf16[3,24,1024]{2,1,0:T(8,128)(2,1)S(1)}, bf16[3,24,1024]{2,1,0:T(8,128)(2,1)S(1)}, u32[]{:S(2)}, u32[]{:S(2)}) collective-permute-start(bf16[3,24,1024]{2,1,0:T(8,128)(2,1)S(1)} %get-tuple-element.25), channel_id=1, source_target_pairs={{0,8},{8,16},{16,24},{24,32},{32,40},{40,48},{48,56},{56,64},{64,7... | collective-permute-start | bytes 442376 | tf_op jit(solution)/shard_map/ppermute | solution.py:20
  12.0 1.3 collective-permute-start.1
  13.3 1.7 collective-permute-done
  15.0 1.0 constant_dynamic-update-slice_fusion.1
  16.0 3.2 %collective-permute-done.1 = bf16[3,24,1024]{2,1,0:T(8,128)(2,1)S(1)} collective-permute-done((bf16[3,24,1024]{2,1,0:T(8,128)(2,1)S(1)}, bf16[3,24,1024]{2,1,0:T(8,128)(2,1)S(1)}, u32[]{:S(2)}, u32[]{:S(2)}) %collective-permute-start.1) | collective-permute-done | bytes 147488 | tf_op jit(solution)/shard_map/ppermute | solution.py:21
  19.3 2.9 %collective-permute-start.3 = (bf16[12,6,1024]{2,1,0:T(8,128)(2,1)S(1)}, bf16[12,6,1024]{2,1,0:T(8,128)(2,1)S(1)}, u32[]{:S(2)}, u32[]{:S(2)}) collective-permute-start(bf16[12,6,1024]{2,1,0:T(8,128)(2,1)S(1)} %get-tuple-element.23), channel_id=1, source_target_pairs={{1,0},{2,1},{3,2},{4,3},{5,4},{6,5},{7,6},{0,7},{9,8},{10,9},{11,1... | collective-permute-start | bytes 442376 | tf_op jit(solution)/shard_map/ppermute | solution.py:21
  22.4 0.1 broadcast_in_dim.31
  22.5 3.2 %collective-permute-done.2 = bf16[12,6,1024]{2,1,0:T(8,128)(2,1)S(1)} collective-permute-done((bf16[12,6,1024]{2,1,0:T(8,128)(2,1)S(1)}, bf16[12,6,1024]{2,1,0:T(8,128)(2,1)S(1)}, u32[]{:S(2)}, u32[]{:S(2)}) %collective-permute-start.2) | collective-permute-done | bytes 147488 | tf_op jit(solution)/shard_map/ppermute | solution.py:20
  25.6 0.4 fusion.58
  26.1 0.1 div.33
  26.2 1.8 multiply_reduce_fusion.1
  28.0 0.1 rsqrt.13
  28.2 1.6 maximum_convert_fusion
  29.8 2.7 reshape.102
  32.5 1.3 fusion.50
  33.8 2.1 fusion.40
  36.0 0.2 pad.4
  36.1 2.1 reshape.99
  38.3 3.2 %copy.47 = bf16[2,3,6,12,1,16,64]{6,5,3,2,1,0,4:T(8,128)(2,1)} copy(bf16[2,3,6,12,1,16,64]{6,5,3,1,2,0,4:T(8,128)(2,1)} %bitcast.60) | data formatting | bytes 1769472 | tf_op jit(solution)/shard_map/transpose | solution.py:42
  41.5 5.5 %fusion.15 = bf16[432,2048]{1,0:T(8,128)(2,1)} fusion(bf16[1024,3072]{1,0:T(8,128)(2,1)} %param.13, f32[432,1024]{1,0:T(8,128)S(1)} %copy-done.3, f32[1024]{0:T(1024)S(1)} %copy-done.6, f32[432]{0:T(512)S(1)} %rsqrt.13, f32[432]{0:T(512)S(1)} %div.33), kind=kOutput, calls=%fused_computation.22 | convolution fusion | flops 1814593536 | bytes 7740800 | tf_op jit(solution)/shard_map/dot_general | solution.py:107
  47.0 6.4 %reshape_reshape.3 = bf16[2,6,3,12,2,16,64]{6,5,4,3,2,1,0:T(8,128)(2,1)} reshape(bf16[432,2048]{1,0:T(8,128)(2,1)} %fusion.15) | data formatting | bytes 3538944 | tf_op jit(solution)/shard_map/reshape;reshape | solution.py:41
  53.4 2.7 copy.45
  56.0 2.6 fusion.59
  58.7 4.1 %copy.59 = bf16[6,72,1,16,64]{1,4,3,0,2:T(8,128)(2,1)} copy(bf16[6,72,1,16,64]{4,3,2,1,0:T(8,128)(2,1)} %get-tuple-element.18) | data formatting | bytes 1769472
  62.7 4.1 %copy.60 = bf16[6,72,1,16,64]{1,4,3,0,2:T(8,128)(2,1)} copy(bf16[6,72,1,16,64]{4,3,2,1,0:T(8,128)(2,1)} %get-tuple-element.19) | data formatting | bytes 1769472
  66.8 3.1 %fusion.25 = f32[6,16,72,72]{2,3,1,0:T(8,128)S(1)} fusion(bf16[6,72,16,64]{3,2,1,0:T(8,128)(2,1)} %bitcast.61, bf16[6,72,1,16,64]{1,4,3,0,2:T(8,128)(2,1)} %copy.60), kind=kOutput, calls=%fused_computation.29 | convolution fusion | flops 63700992 | bytes 3760128 | tf_op jit(solution)/shard_map/wqhd,wkhd->whqk/dot_general | solution.py:53
  69.9 1.8 fusion.62
  71.7 1.9 fusion.34
  73.6 4.0 %copy.51 = bf16[6,72,16,64]{3,2,1,0:T(8,128)(2,1)} copy(bf16[6,72,16,64]{1,3,2,0:T(8,128)(2,1)} %fusion.34) | data formatting | bytes 1769472 | tf_op jit(solution)/shard_map/whqk,wkhd->wqhd/transpose | solution.py:60
  77.6 4.0 %reshape.100 = bf16[2,3,6,12,1024]{4,3,2,1,0:T(8,128)(2,1)} reshape(bf16[6,72,16,64]{3,2,1,0:T(8,128)(2,1)} %copy.51) | data formatting | bytes 1769472 | tf_op jit(solution)/shard_map/reshape | solution.py:62
  81.5 1.4 copy.52
  82.9 1.1 reshape.101
  84.0 1.7 broadcast_in_dim.34
  85.7 2.3 constant_dynamic-update-slice_fusion.10
  88.0 0.7 collective-permute-start.4
  88.8 2.2 collective-permute-start.5
  91.0 0.1 select_reduce_fusion
  91.1 4.3 %collective-permute-done.4 = bf16[6,24,1024]{2,1,0:T(8,128)(2,1)S(1)} collective-permute-done((bf16[6,24,1024]{2,1,0:T(8,128)(2,1)S(1)}, bf16[6,24,1024]{2,1,0:T(8,128)(2,1)S(1)}, u32[]{:S(2)}, u32[]{:S(2)}) %collective-permute-start.4) | collective-permute-done | bytes 294944 | tf_op jit(solution)/shard_map/ppermute | solution.py:143
  95.4 3.0 %collective-permute-start.7 = (bf16[6,24,1024]{2,1,0:T(8,128)(2,1)S(1)}, bf16[6,24,1024]{2,1,0:T(8,128)(2,1)S(1)}, u32[]{:S(2)}, u32[]{:S(2)}) collective-permute-start(bf16[6,24,1024]{2,1,0:T(8,128)(2,1)S(1)} %collective-permute-done.5), channel_id=1, source_target_pairs={{0,7},{1,0},{2,1},{3,2},{4,3},{5,4},{6,5},{7,6},{8,15},{9,8},{10,9... | collective-permute-start | bytes 884744 | tf_op jit(solution)/shard_map/ppermute | solution.py:148
  98.4 0.2 fusion.52
  98.6 4.1 %collective-permute-done.6 = bf16[6,24,1024]{2,1,0:T(8,128)(2,1)S(1)} collective-permute-done((bf16[6,24,1024]{2,1,0:T(8,128)(2,1)S(1)}, bf16[6,24,1024]{2,1,0:T(8,128)(2,1)S(1)}, u32[]{:S(2)}, u32[]{:S(2)}) %collective-permute-start.6) | collective-permute-done | bytes 294944 | tf_op jit(solution)/shard_map/ppermute | solution.py:143
  102.8 0.7 constant_dynamic-update-slice_fusion.9
  103.5 0.7 constant_dynamic-update-slice_fusion.8
  104.3 3.0 %collective-permute-start.9 = (bf16[6,24,1024]{2,1,0:T(8,128)(2,1)S(1)}, bf16[6,24,1024]{2,1,0:T(8,128)(2,1)S(1)}, u32[]{:S(2)}, u32[]{:S(2)}) collective-permute-start(bf16[6,24,1024]{2,1,0:T(8,128)(2,1)S(1)} %collective-permute-done.7), channel_id=1, source_target_pairs={{0,7},{1,0},{2,1},{3,2},{4,3},{5,4},{6,5},{7,6},{8,15},{9,8},{10,9... | collective-permute-start | bytes 884744 | tf_op jit(solution)/shard_map/ppermute | solution.py:148
  107.2 0.8 constant_dynamic-update-slice_fusion.7
  108.0 2.1 collective-permute-done.8
  110.1 0.7 constant_dynamic-update-slice_fusion.6
  110.8 0.7 constant_dynamic-update-slice_fusion.5
  111.6 0.7 constant_dynamic-update-slice_fusion.4
  112.3 5.1 %collective-permute-done.10 = bf16[6,24,1024]{2,1,0:T(8,128)(2,1)S(1)} collective-permute-done((bf16[6,24,1024]{2,1,0:T(8,128)(2,1)S(1)}, bf16[6,24,1024]{2,1,0:T(8,128)(2,1)S(1)}, u32[]{:S(2)}, u32[]{:S(2)}) %collective-permute-start.10) | collective-permute-done | bytes 294944 | tf_op jit(solution)/shard_map/ppermute | solution.py:143
  117.5 0.7 constant_dynamic-update-slice_fusion.3
  118.2 4.3 %convert_element_type.69 = f32[6,192,1024]{2,1,0:T(8,128)} convert(bf16[6,192,1024]{2,1,0:T(8,128)(2,1)} %constant_dynamic-update-slice_fusion.3) | non-fusion elementwise | flops 1179648 | bytes 7077888 | tf_op jit(solution)/shard_map/convert_element_type | solution.py:69
  122.6 9.9 %multiply_convert_fusion = bf16[5,6,192,320]{3,2,1,0:T(8,128)(2,1)S(1)} fusion(bf16[5,6,192,320]{3,2,1,0:T(8,128)(2,1)} %param.18, f32[5,192]{1,0:T(8,128)S(1)} %fusion.52, bf16[5,1024,320]{2,1,0:T(8,128)(2,1)} %all-gather.2.cloned.1.call-done, f32[5,1024]{1,0:T(8,128)S(1)} %copy-done.8, f32[5,1024]{1,0:T(8,128)S(1)} %copy-done.9, ...), kind=kOutput, calls=%fused_computation.11 | convolution fusion | flops 3799941120 | bytes 15412992 | tf_op jit(solution)/shard_map/krnd,kdo->krno/dot_general | solution.py:73
  132.5 2.1 copy-done.13
  134.6 6.6 %fusion.14 = bf16[1024,5,320]{0,2,1:T(8,128)(2,1)} fusion(bf16[5,6,192,320]{3,2,1,0:T(8,128)(2,1)S(1)} %multiply_convert_fusion, f32[5,1024]{1,0:T(8,128)S(1)} %copy-done.8, f32[5,1024]{1,0:T(8,128)S(1)} %copy-done.9, f32[6,192,1024]{2,1,0:T(8,128)S(1)} %copy-done.2), kind=kOutput, calls=%fused_computation.21 | convolution fusion | flops 3795845120 | bytes 11722752 | tf_op jit(solution)/shard_map/krnd,krno->dko/dot_general | solution.py:79
  141.2 9.9 %multiply_reduce_fusion = bf16[6,192,1024]{2,1,0:T(8,128)(2,1)S(1)} fusion(f32[5,1024]{1,0:T(8,128)S(1)} %copy-done.9, bf16[5,6,192,320]{3,2,1,0:T(8,128)(2,1)} %copy-done.13, bf16[5,1024,320]{2,1,0:T(8,128)(2,1)} %all-gather.2.cloned.1.call-done), kind=kOutput, calls=%fused_computation.1 | convolution fusion | flops 3785490432 | bytes 9342976 | tf_op jit(solution)/shard_map/krno,kdo->krnd/dot_general | solution.py:77
  151.1 1.7 copy.61
  152.8 84.8 %all-reduce.3.cloned.1.call-done = bf16[1024,5,320]{0,2,1:T(8,128)(2,1)} async-done(((bf16[1024,5,320]{0,2,1:T(8,128)(2,1)}), bf16[1024,5,320]{0,2,1:T(8,128)(2,1)}) %all-reduce.3.cloned.1.call-update) | async-done | bytes 3276816 | tf_op jit(solution)/shard_map/psum | solution.py:167
  237.7 1.2 convert_bitcast_fusion
  238.8 1.1 copy.53
  239.9 33.6 %reduce-scatter.4.cloned.1.call-done = bf16[24,6144]{1,0:T(8,128)(2,1)} async-done(((bf16[192,6144]{1,0:T(8,128)(2,1)}), bf16[24,6144]{1,0:T(8,128)(2,1)}) %reduce-scatter.4.cloned.1.call-update) | async-done | bytes 294928
  273.5 1.3 reshape.107
  274.9 0.9 copy.58
  (51 shorter events, 0.5 us)
Async XLA Ops:
  7.2 78.5 %copy-start = (bf16[1024,1024]{1,0:T(8,128)(2,1)S(1)}, bf16[1024,1024]{1,0:T(8,128)(2,1)}, u32[]{:S(2)}) copy-start(bf16[1024,1024]{1,0:T(8,128)(2,1)} %param.14) | copy-start | bytes 6291460
  7.2 115.4 %all-gather.2.cloned.1.call-start = ((), (), s32[]{:S(2)}) async-start(), calls=%async_computation.1 | async-start | bytes 4177920 | tf_op jit(solution)/shard_map/all_gather | solution.py:133
  8.4 6.7 %collective-permute-start = (bf16[3,24,1024]{2,1,0:T(8,128)(2,1)S(1)}, bf16[3,24,1024]{2,1,0:T(8,128)(2,1)S(1)}, u32[]{:S(2)}, u32[]{:S(2)}) collective-permute-start(bf16[3,24,1024]{2,1,0:T(8,128)(2,1)S(1)} %get-tuple-element.25), channel_id=1, source_target_pairs={{0,8},{8,16},{16,24},{24,32},{32,40},{40,48},{48,56},{56,64},{64,7... | collective-permute-start | bytes 442376 | tf_op jit(solution)/shard_map/ppermute | solution.py:20
  12.0 225.7 %all-reduce.3.cloned.1.call-start = ((), (), s32[]{:S(2)}) async-start(), calls=%async_computation.2 | async-start | bytes 6553600 | tf_op jit(solution)/shard_map/psum | solution.py:167
  12.0 7.2 %collective-permute-start.1 = (bf16[3,24,1024]{2,1,0:T(8,128)(2,1)S(1)}, bf16[3,24,1024]{2,1,0:T(8,128)(2,1)S(1)}, u32[]{:S(2)}, u32[]{:S(2)}) collective-permute-start(bf16[3,24,1024]{2,1,0:T(8,128)(2,1)S(1)} %get-tuple-element.24), channel_id=1, source_target_pairs={{8,0},{16,8},{24,16},{32,24},{40,32},{48,40},{56,48},{64,56},{72,6... | collective-permute-start | bytes 442376 | tf_op jit(solution)/shard_map/ppermute | solution.py:21
  19.3 6.3 %collective-permute-start.2 = (bf16[12,6,1024]{2,1,0:T(8,128)(2,1)S(1)}, bf16[12,6,1024]{2,1,0:T(8,128)(2,1)S(1)}, u32[]{:S(2)}, u32[]{:S(2)}) collective-permute-start(bf16[12,6,1024]{2,1,0:T(8,128)(2,1)S(1)} %get-tuple-element.22), channel_id=1, source_target_pairs={{0,1},{1,2},{2,3},{3,4},{4,5},{5,6},{6,7},{7,0},{8,9},{9,10},{10,1... | collective-permute-start | bytes 442376 | tf_op jit(solution)/shard_map/ppermute | solution.py:20
  19.3 6.3 %collective-permute-start.3 = (bf16[12,6,1024]{2,1,0:T(8,128)(2,1)S(1)}, bf16[12,6,1024]{2,1,0:T(8,128)(2,1)S(1)}, u32[]{:S(2)}, u32[]{:S(2)}) collective-permute-start(bf16[12,6,1024]{2,1,0:T(8,128)(2,1)S(1)} %get-tuple-element.23), channel_id=1, source_target_pairs={{1,0},{2,1},{3,2},{4,3},{5,4},{6,5},{7,6},{0,7},{9,8},{10,9},{11,1... | collective-permute-start | bytes 442376 | tf_op jit(solution)/shard_map/ppermute | solution.py:21
  29.8 2.7 copy-start.6
  38.3 3.2 %copy-start.3 = (f32[432,1024]{1,0:T(8,128)S(1)}, f32[432,1024]{1,0:T(8,128)}, u32[]{:S(2)}) copy-start(f32[432,1024]{1,0:T(8,128)} %reshape.102) | copy-start | bytes 5308420
  69.9 1.8 copy-start.4
  84.0 1.7 copy-start.5
  85.7 5.3 %copy-start.10 = (s32[4]{0:T(128)S(1)}, s32[4]{0:T(128)}, u32[]{:S(2)}) copy-start(s32[4]{0:T(128)} %param.19) | copy-start | bytes 52
  85.7 5.3 %copy-start.11 = (s32[1,8]{1,0:T(1,128)S(1)}, s32[1,8]{1,0:T(1,128)}, u32[]{:S(2)}) copy-start(s32[1,8]{1,0:T(1,128)} %param.20) | copy-start | bytes 100
  85.7 12.7 %copy-start.12 = (s32[5]{0:T(128)S(1)}, s32[5]{0:T(128)}, u32[]{:S(2)}) copy-start(s32[5]{0:T(128)} %param.21) | copy-start | bytes 64
  88.0 34.5 %copy-start.7 = (bf16[6,24,1024]{2,1,0:T(8,128)(2,1)}, bf16[6,24,1024]{2,1,0:T(8,128)(2,1)S(1)}, u32[]{:S(2)}) copy-start(bf16[6,24,1024]{2,1,0:T(8,128)(2,1)S(1)} %get-tuple-element.29) | copy-start | bytes 884740
  88.0 7.4 %collective-permute-start.4 = (bf16[6,24,1024]{2,1,0:T(8,128)(2,1)S(1)}, bf16[6,24,1024]{2,1,0:T(8,128)(2,1)S(1)}, u32[]{:S(2)}, u32[]{:S(2)}) collective-permute-start(bf16[6,24,1024]{2,1,0:T(8,128)(2,1)S(1)} %get-tuple-element.29), channel_id=1, source_target_pairs={{0,1},{1,2},{2,3},{3,4},{4,5},{5,6},{6,7},{7,0},{8,9},{9,10},{10,1... | collective-permute-start | bytes 884744 | tf_op jit(solution)/shard_map/ppermute | solution.py:143
  88.8 6.6 %collective-permute-start.5 = (bf16[6,24,1024]{2,1,0:T(8,128)(2,1)S(1)}, bf16[6,24,1024]{2,1,0:T(8,128)(2,1)S(1)}, u32[]{:S(2)}, u32[]{:S(2)}) collective-permute-start(bf16[6,24,1024]{2,1,0:T(8,128)(2,1)S(1)} %get-tuple-element.29), channel_id=1, source_target_pairs={{0,7},{1,0},{2,1},{3,2},{4,3},{5,4},{6,5},{7,6},{8,15},{9,8},{10,9... | collective-permute-start | bytes 884744 | tf_op jit(solution)/shard_map/ppermute | solution.py:148
  95.4 7.4 %collective-permute-start.6 = (bf16[6,24,1024]{2,1,0:T(8,128)(2,1)S(1)}, bf16[6,24,1024]{2,1,0:T(8,128)(2,1)S(1)}, u32[]{:S(2)}, u32[]{:S(2)}) collective-permute-start(bf16[6,24,1024]{2,1,0:T(8,128)(2,1)S(1)} %collective-permute-done.4), channel_id=1, source_target_pairs={{0,1},{1,2},{2,3},{3,4},{4,5},{5,6},{6,7},{7,0},{8,9},{9,10},{10,1... | collective-permute-start | bytes 884744 | tf_op jit(solution)/shard_map/ppermute | solution.py:143
  95.4 8.8 %collective-permute-start.7 = (bf16[6,24,1024]{2,1,0:T(8,128)(2,1)S(1)}, bf16[6,24,1024]{2,1,0:T(8,128)(2,1)S(1)}, u32[]{:S(2)}, u32[]{:S(2)}) collective-permute-start(bf16[6,24,1024]{2,1,0:T(8,128)(2,1)S(1)} %collective-permute-done.5), channel_id=1, source_target_pairs={{0,7},{1,0},{2,1},{3,2},{4,3},{5,4},{6,5},{7,6},{8,15},{9,8},{10,9... | collective-permute-start | bytes 884744 | tf_op jit(solution)/shard_map/ppermute | solution.py:148
  102.7 7.4 %collective-permute-start.8 = (bf16[6,24,1024]{2,1,0:T(8,128)(2,1)S(1)}, bf16[6,24,1024]{2,1,0:T(8,128)(2,1)S(1)}, u32[]{:S(2)}, u32[]{:S(2)}) collective-permute-start(bf16[6,24,1024]{2,1,0:T(8,128)(2,1)S(1)} %collective-permute-done.6), channel_id=1, source_target_pairs={{0,1},{1,2},{2,3},{3,4},{4,5},{5,6},{6,7},{7,0},{8,9},{9,10},{10,1... | collective-permute-start | bytes 884744 | tf_op jit(solution)/shard_map/ppermute | solution.py:143
  104.3 7.3 %collective-permute-start.9 = (bf16[6,24,1024]{2,1,0:T(8,128)(2,1)S(1)}, bf16[6,24,1024]{2,1,0:T(8,128)(2,1)S(1)}, u32[]{:S(2)}, u32[]{:S(2)}) collective-permute-start(bf16[6,24,1024]{2,1,0:T(8,128)(2,1)S(1)} %collective-permute-done.7), channel_id=1, source_target_pairs={{0,7},{1,0},{2,1},{3,2},{4,3},{5,4},{6,5},{7,6},{8,15},{9,8},{10,9... | collective-permute-start | bytes 884744 | tf_op jit(solution)/shard_map/ppermute | solution.py:148
  110.1 7.4 %collective-permute-start.10 = (bf16[6,24,1024]{2,1,0:T(8,128)(2,1)S(1)}, bf16[6,24,1024]{2,1,0:T(8,128)(2,1)S(1)}, u32[]{:S(2)}, u32[]{:S(2)}) collective-permute-start(bf16[6,24,1024]{2,1,0:T(8,128)(2,1)S(1)} %collective-permute-done.8), channel_id=1, source_target_pairs={{0,1},{1,2},{2,3},{3,4},{4,5},{5,6},{6,7},{7,0},{8,9},{9,10},{10,1... | collective-permute-start | bytes 884744 | tf_op jit(solution)/shard_map/ppermute | solution.py:143
  118.2 4.3 %copy-start.8 = (f32[5,1024]{1,0:T(8,128)S(1)}, f32[5,1024]{1,0:T(8,128)}, u32[]{:S(2)}) copy-start(f32[5,1024]{1,0:T(8,128)} %param.16) | copy-start | bytes 61444
  118.2 4.3 %copy-start.9 = (f32[5,1024]{1,0:T(8,128)S(1)}, f32[5,1024]{1,0:T(8,128)}, u32[]{:S(2)}) copy-start(f32[5,1024]{1,0:T(8,128)} %param.15) | copy-start | bytes 61444
  122.6 12.0 %copy-start.2 = (f32[6,192,1024]{2,1,0:T(8,128)S(1)}, f32[6,192,1024]{2,1,0:T(8,128)}, u32[]{:S(2)}) copy-start(f32[6,192,1024]{2,1,0:T(8,128)} %convert_element_type.69) | copy-start | bytes 14155780
  132.5 2.1 copy-start.13
  141.2 132.3 %reduce-scatter.4.cloned.1.call-start = ((), (), s32[]{:S(2)}) async-start(), calls=%async_computation.3 | async-start | bytes 2654208
  152.8 123.0 %copy-start.1 = (bf16[1024,1024]{1,0:T(8,128)(2,1)S(1)}, bf16[1024,1024]{1,0:T(8,128)(2,1)}, u32[]{:S(2)}) copy-start(bf16[1024,1024]{1,0:T(8,128)(2,1)} %param.14) | copy-start | bytes 6291460
Sparse Core Ops, SparseCore 0:
  12.1 52.5 all-gather.1
  141.3 96.2 all-reduce.2
  240.2 33.2 reduce-scatter.3
